TPU v7x, 32 devices: a whole 2x2x4 slice. The times are simulated.
32 devices in a mesh: band: 8 (over z, y), rep: 4 (over x, core).
Axes of the slice: x: 2, y: 2, z: 4, core: 2. Of those that a mesh axis runs over, the one named last changes fastest.
Arguments:
- embeddings: bfloat16 [128, 4096], P('rep', 'band'), may hold values from -6 to 6
- route: int32 [4096, 1], P('band'), may hold values from 0 to 7; in each aligned block of 512 rows (0 to 511, 512 to 1023, ...) at most 160 rows name the same one
- place: bfloat16 [2, 4096], P(None, 'band'), may hold values from 0 to 1
- scales: float32 [4], replicated, may hold values from 0.25 to 1
- first_weight: bfloat16 [512, 512], replicated, may hold values from -0.25 to 0.25
- first_bias: float32 [512], replicated, may hold values from -3 to 3
- second_weight: bfloat16 [512, 512], replicated, may hold values from -0.25 to 0.25
- out_cotangent: bfloat16 [512, 96, 256], P(None, ('band', 'rep')), may hold values from -6 to 6
Outputs:
- embed_gradient: float32 [128, 4096], P('rep', 'band')
- first_weight_gradient: float32 [512, 512], replicated
- first_bias_gradient: float32 [512], replicated
- second_weight_gradient: float32 [512, 512], replicated
Inputs may be any that keep to these rules, and one draw needn't show every extreme that they name: `route`: within the 512 reports of one feed (aligned blocks of rows), at most 160 name the same band, and in some block exactly 160 do.
All inputs are finite; a program needn't handle non-finite values.
Results may differ from a plain program's by a relative error of at most 0.0063.
Values may be sent and summed in bfloat16 or wider, within the bound.
No kernel may reach another device: no remote copies, remote signals or barrier semaphores. Data moves between devices by JAX's collectives and lax.ppermute only.
A program may use at most 128 MiB of HBM per device.

v0:
```python
import jax
import jax.numpy as jnp
from jax import lax
from jax.sharding import PartitionSpec as P

root_two_pi = 0.7978845608028654
cubic = 0.044715


def padded(cells, sides, width):
    for axis, dim in sides:
        count = lax.axis_size(axis)
        ends = count - 1
        head = lax.slice_in_dim(cells, 0, width, axis=dim)
        tail = lax.slice_in_dim(cells, cells.shape[dim] - width, cells.shape[dim], axis=dim)
        cells = jnp.concatenate(
            [
                lax.ppermute(tail, axis, [(i, (i + 1) % count) for i in range(ends)]),
                cells,
                lax.ppermute(head, axis, [((i + 1) % count, i) for i in range(ends)]),
            ],
            axis=dim,
        )
    return cells


def gelu_value(value):
    inner = root_two_pi * (value + cubic * value * value * value)
    return 0.5 * value * (1.0 + jnp.tanh(inner))


def gelu_slope(value):
    tangent = jnp.tanh(root_two_pi * (value + cubic * value * value * value))
    return 0.5 * (1.0 + tangent) + 0.5 * value * (1.0 - tangent * tangent) * root_two_pi * (
        1.0 + 3.0 * cubic * value * value
    )


def kernel_factors(geometry, block, scales, lat_rows, columns):
    north_fraction = geometry[0]
    east_fraction = geometry[1]
    valid = geometry[2]
    centre_rows = jnp.arange(lat_rows, dtype=jnp.float32) + 0.5
    north_gap = (
        ((1 - block).astype(jnp.float32) * lat_rows)[None, :]
        + centre_rows[:, None]
        - (north_fraction * lat_rows)[None, :]
    )
    east_gap = (jnp.arange(columns, dtype=jnp.float32) + 0.5)[:, None] - (east_fraction * columns)[
        None, :
    ]
    reach = scales * lat_rows
    inverse = 0.5 / (reach * reach)
    row_kernel = (
        jnp.exp(-(north_gap * north_gap)[None] * inverse[:, None, None]) * valid[None, None, :]
    ).astype(jnp.bfloat16)
    column_kernel = jnp.exp(-(east_gap * east_gap)[None] * inverse[:, None, None]).astype(
        jnp.bfloat16
    )
    return (row_kernel, column_kernel)


def splat(embedded, row_kernel, column_kernel):
    channels = embedded.shape[0]
    levels, lat_rows, slots = row_kernel.shape
    columns = column_kernel.shape[1]
    sums = []
    weights = []
    for level in range(levels):
        weighted = (embedded[:, None, :] * row_kernel[level][None]).reshape(
            channels * lat_rows, slots
        )
        sums.append(
            lax.dot_general(
                weighted,
                column_kernel[level],
                (((1,), (1,)), ((), ())),
                preferred_element_type=jnp.float32,
            )
        )
        weights.append(
            lax.dot_general(
                row_kernel[level],
                column_kernel[level],
                (((1,), (1,)), ((), ())),
                preferred_element_type=jnp.float32,
            )
        )
    splatted = jnp.stack(sums).reshape(levels, channels, lat_rows * columns)
    density = jnp.stack(weights).reshape(levels, lat_rows * columns)
    features = (
        (splatted / (density[:, None, :] + 1.0))
        .transpose(1, 0, 2)
        .reshape(channels * levels, lat_rows * columns)
        .astype(jnp.bfloat16)
    )
    return (features, density)


def spread_back(gradient, row_kernel, column_kernel):
    levels, lat_rows, slots = row_kernel.shape
    columns = column_kernel.shape[1]
    channels = gradient.shape[0] // levels
    grid = gradient.reshape(channels, levels, lat_rows * columns)
    total = jnp.zeros((channels, slots), jnp.float32)
    for level in range(levels):
        slab = grid[:, level].reshape(channels * lat_rows, columns)
        along = jnp.dot(slab, column_kernel[level], preferred_element_type=jnp.float32).reshape(
            channels, lat_rows, slots
        )
        total = total + jnp.sum(along * row_kernel[level][None].astype(jnp.float32), axis=1)
    return total


def band_ranks(route_rows, bands):
    owner = route_rows[:, 0]
    onehot = (owner[:, None] == jnp.arange(bands, dtype=jnp.int32)[None, :]).astype(jnp.int32)
    running = jnp.cumsum(onehot, axis=0)
    return (owner, jnp.sum((running - 1) * onehot, axis=1))


def on_device(
    embeddings, route, place, scales, first_weight, first_bias, second_weight, out_cotangent
):
    channels, reports = embeddings.shape
    bands = lax.axis_size("band")
    parts = lax.axis_size("rep")
    quarter = lax.axis_index("rep")
    capacity = max(2, 5 * reports // (2 * bands))
    sub_rows = out_cotangent.shape[1]
    lat_rows = sub_rows * parts
    columns = out_cotangent.shape[2]
    levels = scales.shape[0]
    owner, rank = band_ranks(route, bands)
    packed = jnp.concatenate([embeddings, place, jnp.ones((1, reports), jnp.bfloat16)], axis=0)
    rows = channels + 3
    whole = bands * capacity
    outgoing = jnp.zeros((rows, whole), jnp.bfloat16).at[:, owner * capacity + rank].set(packed)
    arrived = lax.all_to_all(outgoing, "band", split_axis=1, concat_axis=1, tiled=True)
    nearby = padded(arrived, (("band", 1),), whole)
    block = jnp.arange(3 * whole, dtype=jnp.int32) // whole
    geometry = nearby[channels:].astype(jnp.float32)
    row_kernel, column_kernel = kernel_factors(geometry, block, scales, lat_rows, columns)
    features, density = splat(nearby[:channels], row_kernel, column_kernel)
    cotangent = out_cotangent.reshape(out_cotangent.shape[0], sub_rows * columns)
    mine = lax.all_to_all(features, "rep", split_axis=1, concat_axis=0, tiled=True)
    local_density = lax.dynamic_slice_in_dim(
        density.reshape(levels, lat_rows, columns), quarter * sub_rows, sub_rows, 1
    ).reshape(levels, sub_rows * columns)
    preact = (
        lax.dot_general(
            first_weight, mine, (((0,), (0,)), ((), ())), preferred_element_type=jnp.float32
        )
        + first_bias[:, None]
    )
    hidden = gelu_value(preact).astype(jnp.bfloat16)
    pre_gradient = (
        jnp.dot(second_weight, cotangent, preferred_element_type=jnp.float32) * gelu_slope(preact)
    ).astype(jnp.bfloat16)
    first_sum = lax.dot_general(
        mine, pre_gradient, (((1,), (1,)), ((), ())), preferred_element_type=jnp.float32
    )
    second_sum = lax.dot_general(
        hidden, cotangent, (((1,), (1,)), ((), ())), preferred_element_type=jnp.float32
    )
    bias_sum = jnp.sum(pre_gradient.astype(jnp.float32), axis=1)
    feature_gradient = jnp.dot(first_weight, pre_gradient, preferred_element_type=jnp.float32)
    count = sub_rows * columns
    cell_part = (
        (feature_gradient.reshape(-1, levels, count) / (local_density[None] + 1.0))
        .reshape(-1, count)
        .astype(jnp.bfloat16)
    )
    splat_gradient = lax.all_to_all(cell_part, "rep", split_axis=0, concat_axis=1, tiled=True)
    totals = lax.psum((first_sum, second_sum, bias_sum), ("band", "rep"))
    slot_gradient = spread_back(splat_gradient, row_kernel, column_kernel)
    outward = jnp.concatenate([slot_gradient[:, :whole], slot_gradient[:, 2 * whole :]], axis=1)
    returned = padded(outward, (("band", 1),), whole)
    own_total = slot_gradient[:, whole : 2 * whole] + returned[:, :whole] + returned[:, 3 * whole :]
    backward = lax.all_to_all(own_total, "band", split_axis=1, concat_axis=1, tiled=True)
    embed_gradient = backward[:, owner * capacity + rank]
    return (embed_gradient, totals[0], totals[2], totals[1])


def solution(mesh):
    return jax.shard_map(
        on_device,
        mesh=mesh,
        in_specs=(
            P("rep", "band"),
            P("band", None),
            P(None, "band"),
            P(),
            P(),
            P(),
            P(),
            P(None, ("band", "rep"), None),
        ),
        out_specs=(P("rep", "band"), P(), P(), P()),
        check_vma=False,
    )
```

profile of v0, /device:TPU:0, one launch (start us, length us, event | category | flops | bytes accessed | tf_op | source)
XLA Modules:
  0.0 270.7 jit_solution(15781892218511032208)
XLA Ops:
  14.6 7.3 %all-to-all-start = ((bf16[35,8,160]{2,0,1:T(8,128)(2,1)}), bf16[35,8,160]{2,0,1:T(8,128)(2,1)S(1)}, u32[]{:S(2)}, u32[]{:S(2)}) async-start(bf16[35,8,160]{2,0,1:T(8,128)(2,1)} %copy.50), calls=%async_computation | async-start | bytes 327680 | tf_op jit(solution)/shard_map/all_to_all | solution.py:139
  22.6 6.9 %all-to-all-done = bf16[35,8,160]{2,0,1:T(8,128)(2,1)S(1)} async-done(((bf16[35,8,160]{2,0,1:T(8,128)(2,1)}), bf16[35,8,160]{2,0,1:T(8,128)(2,1)S(1)}, u32[]{:S(2)}, u32[]{:S(2)}) %all-to-all-start) | async-done | bytes 89632 | tf_op jit(solution)/shard_map/all_to_all | solution.py:139
  35.8 3.3 %collective-permute-done.1 = bf16[35,1280]{1,0:T(8,128)(2,1)S(1)} collective-permute-done((bf16[35,1280]{1,0:T(8,128)(2,1)S(1)}, bf16[35,1280]{1,0:T(8,128)(2,1)S(1)}, u32[]{:S(2)}, u32[]{:S(2)}) %collective-permute-start.1) | collective-permute-done | bytes 89632 | tf_op jit(solution)/shard_map/ppermute | solution.py:20
  41.2 2.9 %exponential_convert_fusion = bf16[4,256,3840]{2,1,0:T(8,128)(2,1)S(1)} fusion(f32[4]{0:T(128)S(1)} %multiply_divide_fusion, f32[256,3840]{1,0:T(8,128)S(1)} %multiply_negate_fusion), kind=kLoop, calls=%fused_computation.2 | loop fusion | flops 7864320 | bytes 11796496 | tf_op jit(solution)/shard_map/convert_element_type | solution.py:57
  49.2 6.1 %broadcast_multiply_fusion.3 = (bf16[32,12,3840]{2,1,0:T(8,128)(2,1)}, bf16[32,12,3840]{2,1,0:T(8,128)(2,1)}, bf16[32,12,3840]{2,1,0:T(8,128)(2,1)}, bf16[32,12,3840]{2,1,0:T(8,128)(2,1)}) fusion(bf16[12,3840]{1,0:T(8,128)(2,1)S(1)} %copy-done.10, bf16[32,3840]{1,0:T(8,128)(2,1)S(1)} %slice.107, bf16[12,3840]{1,0:T(8,128)(2,1)S(1)} %copy-done.9, ...), kind=kLoop, calls=%fused_computation.33 | loop fusion | flops 5898240 | bytes 12410880 | tf_op jit(solution)/shard_map/mul | solution.py:70
  55.3 3.9 %mul.295 = bf16[384,3840]{1,0:T(8,128)(2,1)S(1)} reshape(bf16[32,12,3840]{2,1,0:T(8,128)(2,1)} %get-tuple-element.39) | data formatting | bytes 5898240 | tf_op jit(solution)/shard_map/mul | solution.py:70
  59.1 3.2 %fusion.18 = f32[384,256]{1,0:T(8,128)} fusion(bf16[384,3840]{1,0:T(8,128)(2,1)S(1)} %mul.295, bf16[4,256,3840]{2,1,0:T(8,128)(2,1)} %copy-done.1), kind=kOutput, calls=%fused_computation.28 | convolution fusion | flops 754974720 | bytes 5308416 | tf_op jit(solution)/shard_map/dot_general | solution.py:74
  64.5 3.9 %mul.306 = bf16[384,3840]{1,0:T(8,128)(2,1)S(1)} reshape(bf16[32,12,3840]{2,1,0:T(8,128)(2,1)} %get-tuple-element.40) | data formatting | bytes 5898240 | tf_op jit(solution)/shard_map/mul | solution.py:70
  68.4 3.2 %fusion.14 = f32[384,256]{1,0:T(8,128)} fusion(bf16[384,3840]{1,0:T(8,128)(2,1)S(1)} %mul.306, bf16[4,256,3840]{2,1,0:T(8,128)(2,1)} %copy-done.1), kind=kOutput, calls=%fused_computation.24 | convolution fusion | flops 754974720 | bytes 5308416 | tf_op jit(solution)/shard_map/dot_general | solution.py:74
  73.8 3.9 %mul.310 = bf16[384,3840]{1,0:T(8,128)(2,1)S(1)} reshape(bf16[32,12,3840]{2,1,0:T(8,128)(2,1)} %get-tuple-element.41) | data formatting | bytes 5898240 | tf_op jit(solution)/shard_map/mul | solution.py:70
  77.7 3.2 %fusion.10 = f32[384,256]{1,0:T(8,128)} fusion(bf16[384,3840]{1,0:T(8,128)(2,1)S(1)} %mul.310, bf16[4,256,3840]{2,1,0:T(8,128)(2,1)} %copy-done.1), kind=kOutput, calls=%fused_computation.20 | convolution fusion | flops 754974720 | bytes 5308416 | tf_op jit(solution)/shard_map/dot_general | solution.py:74
  83.1 3.9 %mul.314 = bf16[384,3840]{1,0:T(8,128)(2,1)S(1)} reshape(bf16[32,12,3840]{2,1,0:T(8,128)(2,1)} %get-tuple-element.42) | data formatting | bytes 5898240 | tf_op jit(solution)/shard_map/mul | solution.py:70
  87.0 3.3 %fusion.6 = f32[384,256]{1,0:T(8,128)} fusion(bf16[384,3840]{1,0:T(8,128)(2,1)S(1)} %mul.314, bf16[4,256,3840]{2,1,0:T(8,128)(2,1)} %copy-done.1), kind=kOutput, calls=%fused_computation.16 | convolution fusion | flops 754974720 | bytes 5308416 | tf_op jit(solution)/shard_map/dot_general | solution.py:74
  95.9 3.5 %all-to-all-start.1 = ((bf16[128,4,768]{2,0,1:T(8,128)(2,1)}), bf16[128,4,768]{2,0,1:T(8,128)(2,1)S(1)}, u32[]{:S(2)}, u32[]{:S(2)}) async-start(bf16[128,4,768]{2,0,1:T(8,128)(2,1)} %copy.56), calls=%async_computation.1 | async-start | bytes 1572864 | tf_op jit(solution)/shard_map/all_to_all | solution.py:146
  102.6 8.4 %all-to-all-done.1 = bf16[128,4,768]{2,0,1:T(8,128)(2,1)S(1)} async-done(((bf16[128,4,768]{2,0,1:T(8,128)(2,1)}), bf16[128,4,768]{2,0,1:T(8,128)(2,1)S(1)}, u32[]{:S(2)}, u32[]{:S(2)}) %all-to-all-start.1) | async-done | bytes 786464 | tf_op jit(solution)/shard_map/all_to_all | solution.py:146
  115.1 3.5 %all-to-all-start.2 = ((bf16[4,128,768]{2,1,0:T(8,128)(2,1)}), bf16[4,128,768]{2,1,0:T(8,128)(2,1)S(1)}, u32[]{:S(2)}, u32[]{:S(2)}) async-start(bf16[4,128,768]{2,1,0:T(8,128)(2,1)} %bitcast.158), calls=%async_computation.2 | async-start | bytes 1572864 | tf_op jit(solution)/shard_map/all_to_all | solution.py:174
  118.9 2.8 %fusion.90 = f32[512,512]{1,0:T(8,128)} fusion(bf16[512,768]{1,0:T(8,128)(2,1)S(1)} %bitcast.153, bf16[512,768]{1,0:T(8,128)(2,1)} %copy-done.6), kind=kOutput, calls=%fused_computation.140 | convolution fusion | flops 402653184 | bytes 2621440 | tf_op jit(solution)/shard_map/dot_general | solution.py:160
  123.4 6.8 %all-to-all-done.2 = bf16[4,128,768]{2,1,0:T(8,128)(2,1)S(1)} async-done(((bf16[4,128,768]{2,1,0:T(8,128)(2,1)}), bf16[4,128,768]{2,1,0:T(8,128)(2,1)S(1)}, u32[]{:S(2)}, u32[]{:S(2)}) %all-to-all-start.2) | async-done | bytes 786464 | tf_op jit(solution)/shard_map/all_to_all | solution.py:174
  131.2 3.4 %slice_reduce_fusion.2 = (bf16[32,3072]{1,0:T(8,128)(2,1)S(1)}, bf16[32,3072]{1,0:T(8,128)(2,1)S(1)}, bf16[32,3072]{1,0:T(8,128)(2,1)S(1)}, bf16[32,3072]{1,0:T(8,128)(2,1)S(1)}) fusion(bf16[32,4,3072]{2,1,0:T(4,128)(2,1)S(1)} %reshape.284), kind=kLoop, calls=%fused_computation.71 | loop fusion | bytes 1572864 | tf_op jit(solution)/shard_map/slice | solution.py:107
  142.1 3.6 %collective-permute-start.2 = (f32[32,1280]{1,0:T(8,128)S(1)}, f32[32,1280]{1,0:T(8,128)S(1)}, u32[]{:S(2)}, u32[]{:S(2)}) collective-permute-start(f32[32,1280]{1,0:T(8,128)S(1)} %get-tuple-element.29), channel_id=1, source_target_pairs={{0,4},{4,8},{8,12},{12,16},{16,20},{20,24},{24,28},{1,5},{5,9},{9,... | collective-permute-start | bytes 491528 | tf_op jit(solution)/shard_map/ppermute | solution.py:18
  147.0 3.3 %collective-permute-done.2 = f32[32,1280]{1,0:T(8,128)S(1)} collective-permute-done((f32[32,1280]{1,0:T(8,128)S(1)}, f32[32,1280]{1,0:T(8,128)S(1)}, u32[]{:S(2)}, u32[]{:S(2)}) %collective-permute-start.2) | collective-permute-done | bytes 163872 | tf_op jit(solution)/shard_map/ppermute | solution.py:18
  153.9 5.2 %all-to-all-start.3 = ((f32[32,8,160]{2,0,1:T(8,128)}), f32[32,8,160]{2,0,1:T(8,128)S(1)}, u32[]{:S(2)}, u32[]{:S(2)}) async-start(f32[32,8,160]{2,0,1:T(8,128)} %copy.63), calls=%async_computation.3 | async-start | bytes 524288 | tf_op jit(solution)/shard_map/all_to_all | solution.py:180
  159.2 40.6 %psum.22 = f32[512]{0:T(512)} all-reduce(f32[512]{0:T(512)S(1)} %get-tuple-element.43), channel_id=1, replica_groups=mesh['band'=8,'rep'=4] {'band','rep'}, use_global_device_ids=true, to_apply=%region_10.11 | all-reduce | flops 512 | bytes 4096 | tf_op jit(solution)/shard_map/psum | solution.py:175
  201.9 58.7 %all-reduce.3.cloned.1.call-done = (f32[512,512]{1,0:T(8,128)}, f32[512,512]{1,0:T(8,128)}) async-done(((f32[512,512]{1,0:T(8,128)}, f32[512,512]{1,0:T(8,128)}), (f32[512,512]{1,0:T(8,128)}, f32[512,512]{1,0:T(8,128)})) %all-reduce.3.cloned.1.call-update) | async-done | bytes 2097168 | tf_op jit(solution)/shard_map/psum | solution.py:175
  (131 shorter events, 61.1 us)
Async XLA Ops:
  7.2 103.8 %copy-start = (bf16[512,512]{1,0:T(8,128)(2,1)S(1)}, bf16[512,512]{1,0:T(8,128)(2,1)}, u32[]{:S(2)}) copy-start(bf16[512,512]{1,0:T(8,128)(2,1)} %param.12) | copy-start | bytes 1572868
  10.8 28.9 %copy-start.18 = (s32[512,1]{0,1:T(1,128)}, s32[512,1]{0,1:T(1,128)S(1)}, u32[]{:S(2)}) copy-start(s32[512,1]{0,1:T(1,128)S(1)} %compare_select_fusion) | copy-start | bytes 6148
  14.6 14.9 %all-to-all-start = ((bf16[35,8,160]{2,0,1:T(8,128)(2,1)}), bf16[35,8,160]{2,0,1:T(8,128)(2,1)S(1)}, u32[]{:S(2)}, u32[]{:S(2)}) async-start(bf16[35,8,160]{2,0,1:T(8,128)(2,1)} %copy.50), calls=%async_computation | async-start | bytes 327680 | tf_op jit(solution)/shard_map/all_to_all | solution.py:139
  29.7 6.1 %collective-permute-start = (bf16[35,1280]{1,0:T(8,128)(2,1)S(1)}, bf16[35,1280]{1,0:T(8,128)(2,1)S(1)}, u32[]{:S(2)}, u32[]{:S(2)}) collective-permute-start(bf16[35,1280]{1,0:T(8,128)(2,1)S(1)} %all_to_all.42), channel_id=1, source_target_pairs={{0,4},{4,8},{8,12},{12,16},{16,20},{20,24},{24,28},{1,5},{5,9},{9,... | collective-permute-start | bytes 268808 | tf_op jit(solution)/shard_map/ppermute | solution.py:18
  32.6 6.6 %collective-permute-start.1 = (bf16[35,1280]{1,0:T(8,128)(2,1)S(1)}, bf16[35,1280]{1,0:T(8,128)(2,1)S(1)}, u32[]{:S(2)}, u32[]{:S(2)}) collective-permute-start(bf16[35,1280]{1,0:T(8,128)(2,1)S(1)} %all_to_all.42), channel_id=1, source_target_pairs={{4,0},{8,4},{12,8},{16,12},{20,16},{24,20},{28,24},{5,1},{9,5},{13... | collective-permute-start | bytes 268808 | tf_op jit(solution)/shard_map/ppermute | solution.py:20
  44.2 11.1 %copy-start.1 = (bf16[4,256,3840]{2,1,0:T(8,128)(2,1)}, bf16[4,256,3840]{2,1,0:T(8,128)(2,1)S(1)}, u32[]{:S(2)}) copy-start(bf16[4,256,3840]{2,1,0:T(8,128)(2,1)S(1)} %exponential_convert_fusion) | copy-start | bytes 23592964
  87.0 4.7 %copy-start.15 = (f32[12,256]{1,0:T(8,128)S(1)}, f32[12,256]{1,0:T(8,128)}, u32[]{:S(2)}) copy-start(f32[12,256]{1,0:T(8,128)} %fusion.8) | copy-start | bytes 36868
  87.0 4.7 %copy-start.16 = (f32[12,256]{1,0:T(8,128)S(1)}, f32[12,256]{1,0:T(8,128)}, u32[]{:S(2)}) copy-start(f32[12,256]{1,0:T(8,128)} %fusion.12) | copy-start | bytes 36868
  87.0 4.8 %copy-start.17 = (f32[12,256]{1,0:T(8,128)S(1)}, f32[12,256]{1,0:T(8,128)}, u32[]{:S(2)}) copy-start(f32[12,256]{1,0:T(8,128)} %fusion.16) | copy-start | bytes 36868
  94.9 4.5 %copy-start.4 = (bf16[512,3,256]{2,0,1:T(8,128)(2,1)S(1)}, bf16[512,3,256]{2,0,1:T(8,128)(2,1)}, u32[]{:S(2)}) copy-start(bf16[512,3,256]{2,0,1:T(8,128)(2,1)} %param.15) | copy-start | bytes 2359300
  95.9 15.1 %all-to-all-start.1 = ((bf16[128,4,768]{2,0,1:T(8,128)(2,1)}), bf16[128,4,768]{2,0,1:T(8,128)(2,1)S(1)}, u32[]{:S(2)}, u32[]{:S(2)}) async-start(bf16[128,4,768]{2,0,1:T(8,128)(2,1)} %copy.56), calls=%async_computation.1 | async-start | bytes 1572864 | tf_op jit(solution)/shard_map/all_to_all | solution.py:146
  100.8 10.2 %copy-start.21 = (f32[512]{0:T(512)S(1)}, f32[512]{0:T(512)}, u32[]{:S(2)}) copy-start(f32[512]{0:T(512)} %param.13) | copy-start | bytes 6148
  102.6 9.1 %copy-start.5 = (bf16[512,3,256]{0,2,1:T(8,128)(2,1)S(1)}, bf16[512,3,256]{0,2,1:T(8,128)(2,1)}, u32[]{:S(2)}) copy-start(bf16[512,3,256]{0,2,1:T(8,128)(2,1)} %copy.48) | copy-start | bytes 2359300
  102.6 9.1 %copy-start.20 = (bf16[512,512]{1,0:T(8,128)(2,1)S(1)}, bf16[512,512]{1,0:T(8,128)(2,1)}, u32[]{:S(2)}) copy-start(bf16[512,512]{1,0:T(8,128)(2,1)} %param.14) | copy-start | bytes 1572868
  115.1 15.1 %all-to-all-start.2 = ((bf16[4,128,768]{2,1,0:T(8,128)(2,1)}), bf16[4,128,768]{2,1,0:T(8,128)(2,1)S(1)}, u32[]{:S(2)}, u32[]{:S(2)}) async-start(bf16[4,128,768]{2,1,0:T(8,128)(2,1)} %bitcast.158), calls=%async_computation.2 | async-start | bytes 1572864 | tf_op jit(solution)/shard_map/all_to_all | solution.py:174
  118.6 141.9 %all-reduce.3.cloned.1.call-start = ((), (), s32[]{:S(2)}) async-start(), calls=%async_computation.4 | async-start | bytes 4194304 | tf_op jit(solution)/shard_map/psum | solution.py:175
  118.9 2.8 %copy-start.23 = (f32[768,512]{0,1:T(8,128)S(1)}, f32[768,512]{0,1:T(8,128)}, u32[]{:S(2)}) copy-start(f32[768,512]{0,1:T(8,128)} %copy-done.22) | copy-start | bytes 4718596
  130.8 3.7 %copy-start.14 = (f32[12,3840]{1,0:T(8,128)S(1)}, f32[12,3840]{1,0:T(8,128)}, u32[]{:S(2)}) copy-start(f32[12,3840]{1,0:T(8,128)} %get-tuple-element.31) | copy-start | bytes 552964
  131.1 8.8 %slice-start = ((s8[7864320]{0:T(1024)(128)(4,1)}), s8[3670016]{0:T(1024)(128)(4,1)S(1)}, s32[]{:S(2)}) async-start(s8[7864320]{0:T(1024)(128)(4,1)} %bitcast.149), calls=%async_computation.5 | async-start | bytes 7340032
  134.6 5.4 %slice-start.1 = ((s8[7864320]{0:T(1024)(128)(4,1)}), s8[4194304]{0:T(1024)(128)(4,1)S(1)}, s32[]{:S(2)}) async-start(s8[7864320]{0:T(1024)(128)(4,1)} %bitcast.149), calls=%async_computation.6 | async-start | bytes 8388608
  142.0 17.1 %copy-start.19 = (s32[512,1]{0,1:T(1,128)S(1)}, s32[512,1]{0,1:T(1,128)}, u32[]{:S(2)}) copy-start(s32[512,1]{0,1:T(1,128)} %copy-done.18) | copy-start | bytes 6148
  142.1 8.3 %collective-permute-start.2 = (f32[32,1280]{1,0:T(8,128)S(1)}, f32[32,1280]{1,0:T(8,128)S(1)}, u32[]{:S(2)}, u32[]{:S(2)}) collective-permute-start(f32[32,1280]{1,0:T(8,128)S(1)} %get-tuple-element.29), channel_id=1, source_target_pairs={{0,4},{4,8},{8,12},{12,16},{16,20},{20,24},{24,28},{1,5},{5,9},{9,... | collective-permute-start | bytes 491528 | tf_op jit(solution)/shard_map/ppermute | solution.py:18
  145.7 7.3 %collective-permute-start.3 = (f32[32,1280]{1,0:T(8,128)S(1)}, f32[32,1280]{1,0:T(8,128)S(1)}, u32[]{:S(2)}, u32[]{:S(2)}) collective-permute-start(f32[32,1280]{1,0:T(8,128)S(1)} %get-tuple-element.30), channel_id=1, source_target_pairs={{4,0},{8,4},{12,8},{16,12},{20,16},{24,20},{28,24},{5,1},{9,5},{13... | collective-permute-start | bytes 491528 | tf_op jit(solution)/shard_map/ppermute | solution.py:20
  153.9 45.9 %all-to-all-start.3 = ((f32[32,8,160]{2,0,1:T(8,128)}), f32[32,8,160]{2,0,1:T(8,128)S(1)}, u32[]{:S(2)}, u32[]{:S(2)}) async-start(f32[32,8,160]{2,0,1:T(8,128)} %copy.63), calls=%async_computation.3 | async-start | bytes 524288 | tf_op jit(solution)/shard_map/all_to_all | solution.py:180
  (11 other events, 24.3 us)
Sparse Core Ops, SparseCore 0:
  125.5 134.9 all-reduce.2
where the time goes:
time: 272 us; the launch traced here: 271 us
  waiting for transfers between devices  92.1 us (34%)
  local copies, waits for them, and re-layouts  42.5 us (16%)
  blocking collectives  40.6 us (15%)
  matrix products  33.1 us (12%)
  starting transfers between devices  28.8 us (11%)
  other arithmetic  18.9 us (7%)
  between operations  14.7 us (5%)
    psum x1, waiting for transfers between devices, on_device(): totals = lax.psum((first_sum, second_sum, bias_sum), ('band', 'rep'))  58.7 us
    psum x1, blocking collectives, on_device(): totals = lax.psum((first_sum, second_sum, bias_sum), ('band', 'rep'))  40.6 us
    mul x4, local copies, waits for them, and re-layouts, splat(): embedded[:, None, :] * row_kernel[level][None]  15.5 us
    dot_general x4, matrix products, splat(): lax.dot_general(weighted, column_kernel[level], (((1,), (1,)), ((), ())),...  13 us
    all_to_all x1, waiting for transfers between devices, on_device(): lax.all_to_all(features, 'rep', split_axis=1, concat_axis=0, tiled=True)  8.44 us
    another operation x4, local copies, waits for them, and re-layouts, splat(): splatted = jnp.stack(sums).reshape(levels, channels, lat_rows * columns)  7.83 us
    all_to_all x1, starting transfers between devices, on_device(): lax.all_to_all(outgoing, 'band', split_axis=1, concat_axis=1, tiled=True)  7.31 us
    dot_general x4, matrix products, spread_back(): jnp.dot(slab, column_kernel[level], preferred_element_type=jnp.float32)  7.24 us
  transfers between devices with their start and end apart: 9, of which 8 were waited for; matrix products, arithmetic and copies ran while one was open for 8% of the time, Pallas kernels for 0%

commit v1 on v0

--- a/solution.py
+++ b/solution.py
@@ -136,7 +136,10 @@
     rows = channels + 3
     whole = bands * capacity
     outgoing = jnp.zeros((rows, whole), jnp.bfloat16).at[:, owner * capacity + rank].set(packed)
-    arrived = lax.all_to_all(outgoing, "band", split_axis=1, concat_axis=1, tiled=True)
+    arrived = jnp.concatenate(
+        lax.all_to_all(jnp.stack(jnp.split(outgoing, lax.axis_size("band"), axis=1)), "band", 0, 0),
+        axis=1,
+    )
     nearby = padded(arrived, (("band", 1),), whole)
     block = jnp.arange(3 * whole, dtype=jnp.int32) // whole
     geometry = nearby[channels:].astype(jnp.float32)

time: 272 us -> 272 us (level)
    unnamed x63 -> x72, local copies, waits for them, and re-layouts: 6.03 us -> 6.12 us
where the time goes in v1:
time: 272 us; the launch traced here: 271 us
  waiting for transfers between devices  92.7 us (34%)
  local copies, waits for them, and re-layouts  42.6 us (16%)
  blocking collectives  40.6 us (15%)
  matrix products  33.1 us (12%)
  starting transfers between devices  28.8 us (11%)
  other arithmetic  18.3 us (7%)
  between operations  14.7 us (5%)
    psum x1, waiting for transfers between devices, on_device(): totals = lax.psum((first_sum, second_sum, bias_sum), ('band', 'rep'))  58.7 us
    psum x1, blocking collectives, on_device(): totals = lax.psum((first_sum, second_sum, bias_sum), ('band', 'rep'))  40.6 us
    mul x4, local copies, waits for them, and re-layouts, splat(): embedded[:, None, :] * row_kernel[level][None]  15.5 us
    dot_general x4, matrix products, splat(): lax.dot_general(weighted, column_kernel[level], (((1,), (1,)), ((), ())),...  13 us
    all_to_all x1, waiting for transfers between devices, on_device(): lax.all_to_all(features, 'rep', split_axis=1, concat_axis=0, tiled=True)  8.44 us
    another operation x4, local copies, waits for them, and re-layouts, splat(): splatted = jnp.stack(sums).reshape(levels, channels, lat_rows * columns)  7.83 us
    all_to_all x1, waiting for transfers between devices, on_device(): lax.all_to_all(jnp.stack(jnp.split(outgoing, lax.axis_size('band'), axis=...  7.51 us
    all_to_all x1, starting transfers between devices, on_device(): lax.all_to_all(jnp.stack(jnp.split(outgoing, lax.axis_size('band'), axis=...  7.31 us
  transfers between devices with their start and end apart: 9, of which 8 were waited for; matrix products, arithmetic and copies ran while one was open for 8% of the time, Pallas kernels for 0%

profile of v1, /device:TPU:0, one launch (start us, length us, event | category | flops | bytes accessed | tf_op | source)
XLA Modules:
  0.0 270.9 jit_solution(7669994787686533595)
XLA Ops:
  14.8 7.3 %all-to-all-start = ((bf16[8,35,160]{2,1,0:T(8,128)(2,1)}), bf16[8,35,160]{2,1,0:T(8,128)(2,1)S(1)}, u32[]{:S(2)}, u32[]{:S(2)}) async-start(bf16[8,35,160]{2,1,0:T(8,128)(2,1)} %copy.86), calls=%async_computation | async-start | bytes 327680 | tf_op jit(solution)/shard_map/all_to_all | solution.py:140
  22.1 7.5 %all-to-all-done = bf16[8,35,160]{2,1,0:T(8,128)(2,1)S(1)} async-done(((bf16[8,35,160]{2,1,0:T(8,128)(2,1)}), bf16[8,35,160]{2,1,0:T(8,128)(2,1)S(1)}, u32[]{:S(2)}, u32[]{:S(2)}) %all-to-all-start) | async-done | bytes 89632 | tf_op jit(solution)/shard_map/all_to_all | solution.py:140
  36.0 3.3 %collective-permute-done.1 = bf16[35,1280]{1,0:T(8,128)(2,1)S(1)} collective-permute-done((bf16[35,1280]{1,0:T(8,128)(2,1)S(1)}, bf16[35,1280]{1,0:T(8,128)(2,1)S(1)}, u32[]{:S(2)}, u32[]{:S(2)}) %collective-permute-start.1) | collective-permute-done | bytes 89632 | tf_op jit(solution)/shard_map/ppermute | solution.py:20
  41.3 2.9 %exponential_convert_fusion = bf16[4,256,3840]{2,1,0:T(8,128)(2,1)S(1)} fusion(f32[4]{0:T(128)S(1)} %multiply_divide_fusion, f32[256,3840]{1,0:T(8,128)S(1)} %multiply_negate_fusion), kind=kLoop, calls=%fused_computation.2 | loop fusion | flops 7864320 | bytes 11796496 | tf_op jit(solution)/shard_map/convert_element_type | solution.py:57
  49.3 6.1 %broadcast_multiply_fusion.3 = (bf16[32,12,3840]{2,1,0:T(8,128)(2,1)}, bf16[32,12,3840]{2,1,0:T(8,128)(2,1)}, bf16[32,12,3840]{2,1,0:T(8,128)(2,1)}, bf16[32,12,3840]{2,1,0:T(8,128)(2,1)}) fusion(bf16[12,3840]{1,0:T(8,128)(2,1)S(1)} %copy-done.10, bf16[32,3840]{1,0:T(8,128)(2,1)S(1)} %slice.107, bf16[12,3840]{1,0:T(8,128)(2,1)S(1)} %copy-done.9, ...), kind=kLoop, calls=%fused_computation.33 | loop fusion | flops 5898240 | bytes 12410880 | tf_op jit(solution)/shard_map/mul | solution.py:70
  55.4 3.9 %mul.295 = bf16[384,3840]{1,0:T(8,128)(2,1)S(1)} reshape(bf16[32,12,3840]{2,1,0:T(8,128)(2,1)} %get-tuple-element.43) | data formatting | bytes 5898240 | tf_op jit(solution)/shard_map/mul | solution.py:70
  59.3 3.3 %fusion.18 = f32[384,256]{1,0:T(8,128)} fusion(bf16[384,3840]{1,0:T(8,128)(2,1)S(1)} %mul.295, bf16[4,256,3840]{2,1,0:T(8,128)(2,1)} %copy-done.1), kind=kOutput, calls=%fused_computation.28 | convolution fusion | flops 754974720 | bytes 5308416 | tf_op jit(solution)/shard_map/dot_general | solution.py:74
  64.7 3.9 %mul.306 = bf16[384,3840]{1,0:T(8,128)(2,1)S(1)} reshape(bf16[32,12,3840]{2,1,0:T(8,128)(2,1)} %get-tuple-element.44) | data formatting | bytes 5898240 | tf_op jit(solution)/shard_map/mul | solution.py:70
  68.6 3.3 %fusion.14 = f32[384,256]{1,0:T(8,128)} fusion(bf16[384,3840]{1,0:T(8,128)(2,1)S(1)} %mul.306, bf16[4,256,3840]{2,1,0:T(8,128)(2,1)} %copy-done.1), kind=kOutput, calls=%fused_computation.24 | convolution fusion | flops 754974720 | bytes 5308416 | tf_op jit(solution)/shard_map/dot_general | solution.py:74
  74.0 3.9 %mul.310 = bf16[384,3840]{1,0:T(8,128)(2,1)S(1)} reshape(bf16[32,12,3840]{2,1,0:T(8,128)(2,1)} %get-tuple-element.45) | data formatting | bytes 5898240 | tf_op jit(solution)/shard_map/mul | solution.py:70
  77.9 3.3 %fusion.10 = f32[384,256]{1,0:T(8,128)} fusion(bf16[384,3840]{1,0:T(8,128)(2,1)S(1)} %mul.310, bf16[4,256,3840]{2,1,0:T(8,128)(2,1)} %copy-done.1), kind=kOutput, calls=%fused_computation.20 | convolution fusion | flops 754974720 | bytes 5308416 | tf_op jit(solution)/shard_map/dot_general | solution.py:74
  83.3 3.9 %mul.314 = bf16[384,3840]{1,0:T(8,128)(2,1)S(1)} reshape(bf16[32,12,3840]{2,1,0:T(8,128)(2,1)} %get-tuple-element.46) | data formatting | bytes 5898240 | tf_op jit(solution)/shard_map/mul | solution.py:70
  87.2 3.3 %fusion.6 = f32[384,256]{1,0:T(8,128)} fusion(bf16[384,3840]{1,0:T(8,128)(2,1)S(1)} %mul.314, bf16[4,256,3840]{2,1,0:T(8,128)(2,1)} %copy-done.1), kind=kOutput, calls=%fused_computation.16 | convolution fusion | flops 754974720 | bytes 5308416 | tf_op jit(solution)/shard_map/dot_general | solution.py:74
  96.1 3.5 %all-to-all-start.1 = ((bf16[128,4,768]{2,0,1:T(8,128)(2,1)}), bf16[128,4,768]{2,0,1:T(8,128)(2,1)S(1)}, u32[]{:S(2)}, u32[]{:S(2)}) async-start(bf16[128,4,768]{2,0,1:T(8,128)(2,1)} %copy.92), calls=%async_computation.1 | async-start | bytes 1572864 | tf_op jit(solution)/shard_map/all_to_all | solution.py:149
  102.7 8.4 %all-to-all-done.1 = bf16[128,4,768]{2,0,1:T(8,128)(2,1)S(1)} async-done(((bf16[128,4,768]{2,0,1:T(8,128)(2,1)}), bf16[128,4,768]{2,0,1:T(8,128)(2,1)S(1)}, u32[]{:S(2)}, u32[]{:S(2)}) %all-to-all-start.1) | async-done | bytes 786464 | tf_op jit(solution)/shard_map/all_to_all | solution.py:149
  115.3 3.5 %all-to-all-start.2 = ((bf16[4,128,768]{2,1,0:T(8,128)(2,1)}), bf16[4,128,768]{2,1,0:T(8,128)(2,1)S(1)}, u32[]{:S(2)}, u32[]{:S(2)}) async-start(bf16[4,128,768]{2,1,0:T(8,128)(2,1)} %bitcast.189), calls=%async_computation.2 | async-start | bytes 1572864 | tf_op jit(solution)/shard_map/all_to_all | solution.py:177
  119.1 2.8 %fusion.98 = f32[512,512]{1,0:T(8,128)} fusion(bf16[512,768]{1,0:T(8,128)(2,1)S(1)} %bitcast.185, bf16[512,768]{1,0:T(8,128)(2,1)} %copy-done.6), kind=kOutput, calls=%fused_computation.156 | convolution fusion | flops 402653184 | bytes 2621440 | tf_op jit(solution)/shard_map/dot_general | solution.py:163
  123.5 6.8 %all-to-all-done.2 = bf16[4,128,768]{2,1,0:T(8,128)(2,1)S(1)} async-done(((bf16[4,128,768]{2,1,0:T(8,128)(2,1)}), bf16[4,128,768]{2,1,0:T(8,128)(2,1)S(1)}, u32[]{:S(2)}, u32[]{:S(2)}) %all-to-all-start.2) | async-done | bytes 786464 | tf_op jit(solution)/shard_map/all_to_all | solution.py:177
  131.3 3.4 %slice_reduce_fusion.2 = (bf16[32,3072]{1,0:T(8,128)(2,1)S(1)}, bf16[32,3072]{1,0:T(8,128)(2,1)S(1)}, bf16[32,3072]{1,0:T(8,128)(2,1)S(1)}, bf16[32,3072]{1,0:T(8,128)(2,1)S(1)}) fusion(bf16[32,4,3072]{2,1,0:T(4,128)(2,1)S(1)} %reshape.290), kind=kLoop, calls=%fused_computation.71 | loop fusion | bytes 1572864 | tf_op jit(solution)/shard_map/slice | solution.py:107
  142.2 3.6 %collective-permute-start.2 = (f32[32,1280]{1,0:T(8,128)S(1)}, f32[32,1280]{1,0:T(8,128)S(1)}, u32[]{:S(2)}, u32[]{:S(2)}) collective-permute-start(f32[32,1280]{1,0:T(8,128)S(1)} %get-tuple-element.33), channel_id=1, source_target_pairs={{0,4},{4,8},{8,12},{12,16},{16,20},{20,24},{24,28},{1,5},{5,9},{9,... | collective-permute-start | bytes 491528 | tf_op jit(solution)/shard_map/ppermute | solution.py:18
  147.2 3.3 %collective-permute-done.2 = f32[32,1280]{1,0:T(8,128)S(1)} collective-permute-done((f32[32,1280]{1,0:T(8,128)S(1)}, f32[32,1280]{1,0:T(8,128)S(1)}, u32[]{:S(2)}, u32[]{:S(2)}) %collective-permute-start.2) | collective-permute-done | bytes 163872 | tf_op jit(solution)/shard_map/ppermute | solution.py:18
  154.1 5.2 %all-to-all-start.3 = ((f32[32,8,160]{2,0,1:T(8,128)}), f32[32,8,160]{2,0,1:T(8,128)S(1)}, u32[]{:S(2)}, u32[]{:S(2)}) async-start(f32[32,8,160]{2,0,1:T(8,128)} %copy.99), calls=%async_computation.3 | async-start | bytes 524288 | tf_op jit(solution)/shard_map/all_to_all | solution.py:183
  159.3 40.6 %psum.22 = f32[512]{0:T(512)} all-reduce(f32[512]{0:T(512)S(1)} %get-tuple-element.47), channel_id=1, replica_groups=mesh['band'=8,'rep'=4] {'band','rep'}, use_global_device_ids=true, to_apply=%region_10.11 | all-reduce | flops 512 | bytes 4096 | tf_op jit(solution)/shard_map/psum | solution.py:178
  202.0 58.7 %all-reduce.3.cloned.1.call-done = (f32[512,512]{1,0:T(8,128)}, f32[512,512]{1,0:T(8,128)}) async-done(((f32[512,512]{1,0:T(8,128)}, f32[512,512]{1,0:T(8,128)}), (f32[512,512]{1,0:T(8,128)}, f32[512,512]{1,0:T(8,128)})) %all-reduce.3.cloned.1.call-update) | async-done | bytes 2097168 | tf_op jit(solution)/shard_map/psum | solution.py:178
  (141 shorter events, 60.5 us)
Async XLA Ops:
  7.2 104.0 %copy-start = (bf16[512,512]{1,0:T(8,128)(2,1)S(1)}, bf16[512,512]{1,0:T(8,128)(2,1)}, u32[]{:S(2)}) copy-start(bf16[512,512]{1,0:T(8,128)(2,1)} %param.12) | copy-start | bytes 1572868
  7.2 14.9 %copy-start.22 = (f32[4]{0:T(128)S(1)}, f32[4]{0:T(128)}, u32[]{:S(2)}) copy-start(f32[4]{0:T(128)} %param.11) | copy-start | bytes 52
  14.8 14.9 %all-to-all-start = ((bf16[8,35,160]{2,1,0:T(8,128)(2,1)}), bf16[8,35,160]{2,1,0:T(8,128)(2,1)S(1)}, u32[]{:S(2)}, u32[]{:S(2)}) async-start(bf16[8,35,160]{2,1,0:T(8,128)(2,1)} %copy.86), calls=%async_computation | async-start | bytes 327680 | tf_op jit(solution)/shard_map/all_to_all | solution.py:140
  29.9 6.1 %collective-permute-start = (bf16[35,1280]{1,0:T(8,128)(2,1)S(1)}, bf16[35,1280]{1,0:T(8,128)(2,1)S(1)}, u32[]{:S(2)}, u32[]{:S(2)}) collective-permute-start(bf16[35,1280]{1,0:T(8,128)(2,1)S(1)} %reshape.289), channel_id=1, source_target_pairs={{0,4},{4,8},{8,12},{12,16},{16,20},{20,24},{24,28},{1,5},{5,9},{9,... | collective-permute-start | bytes 268808 | tf_op jit(solution)/shard_map/ppermute | solution.py:18
  32.7 6.6 %collective-permute-start.1 = (bf16[35,1280]{1,0:T(8,128)(2,1)S(1)}, bf16[35,1280]{1,0:T(8,128)(2,1)S(1)}, u32[]{:S(2)}, u32[]{:S(2)}) collective-permute-start(bf16[35,1280]{1,0:T(8,128)(2,1)S(1)} %reshape.289), channel_id=1, source_target_pairs={{4,0},{8,4},{12,8},{16,12},{20,16},{24,20},{28,24},{5,1},{9,5},{13... | collective-permute-start | bytes 268808 | tf_op jit(solution)/shard_map/ppermute | solution.py:20
  44.3 11.1 %copy-start.1 = (bf16[4,256,3840]{2,1,0:T(8,128)(2,1)}, bf16[4,256,3840]{2,1,0:T(8,128)(2,1)S(1)}, u32[]{:S(2)}) copy-start(bf16[4,256,3840]{2,1,0:T(8,128)(2,1)S(1)} %exponential_convert_fusion) | copy-start | bytes 23592964
  87.1 4.7 %copy-start.15 = (f32[12,256]{1,0:T(8,128)S(1)}, f32[12,256]{1,0:T(8,128)}, u32[]{:S(2)}) copy-start(f32[12,256]{1,0:T(8,128)} %fusion.8) | copy-start | bytes 36868
  87.2 4.7 %copy-start.16 = (f32[12,256]{1,0:T(8,128)S(1)}, f32[12,256]{1,0:T(8,128)}, u32[]{:S(2)}) copy-start(f32[12,256]{1,0:T(8,128)} %fusion.12) | copy-start | bytes 36868
  87.2 4.8 %copy-start.17 = (f32[12,256]{1,0:T(8,128)S(1)}, f32[12,256]{1,0:T(8,128)}, u32[]{:S(2)}) copy-start(f32[12,256]{1,0:T(8,128)} %fusion.16) | copy-start | bytes 36868
  95.1 4.5 %copy-start.4 = (bf16[512,3,256]{2,0,1:T(8,128)(2,1)S(1)}, bf16[512,3,256]{2,0,1:T(8,128)(2,1)}, u32[]{:S(2)}) copy-start(bf16[512,3,256]{2,0,1:T(8,128)(2,1)} %param.15) | copy-start | bytes 2359300
  96.1 15.1 %all-to-all-start.1 = ((bf16[128,4,768]{2,0,1:T(8,128)(2,1)}), bf16[128,4,768]{2,0,1:T(8,128)(2,1)S(1)}, u32[]{:S(2)}, u32[]{:S(2)}) async-start(bf16[128,4,768]{2,0,1:T(8,128)(2,1)} %copy.92), calls=%async_computation.1 | async-start | bytes 1572864 | tf_op jit(solution)/shard_map/all_to_all | solution.py:149
  101.0 10.2 %copy-start.21 = (f32[512]{0:T(512)S(1)}, f32[512]{0:T(512)}, u32[]{:S(2)}) copy-start(f32[512]{0:T(512)} %param.13) | copy-start | bytes 6148
  102.7 9.1 %copy-start.5 = (bf16[512,3,256]{0,2,1:T(8,128)(2,1)S(1)}, bf16[512,3,256]{0,2,1:T(8,128)(2,1)}, u32[]{:S(2)}) copy-start(bf16[512,3,256]{0,2,1:T(8,128)(2,1)} %copy.84) | copy-start | bytes 2359300
  102.7 9.1 %copy-start.20 = (bf16[512,512]{1,0:T(8,128)(2,1)S(1)}, bf16[512,512]{1,0:T(8,128)(2,1)}, u32[]{:S(2)}) copy-start(bf16[512,512]{1,0:T(8,128)(2,1)} %param.14) | copy-start | bytes 1572868
  115.3 15.1 %all-to-all-start.2 = ((bf16[4,128,768]{2,1,0:T(8,128)(2,1)}), bf16[4,128,768]{2,1,0:T(8,128)(2,1)S(1)}, u32[]{:S(2)}, u32[]{:S(2)}) async-start(bf16[4,128,768]{2,1,0:T(8,128)(2,1)} %bitcast.189), calls=%async_computation.2 | async-start | bytes 1572864 | tf_op jit(solution)/shard_map/all_to_all | solution.py:177
  118.8 141.9 %all-reduce.3.cloned.1.call-start = ((), (), s32[]{:S(2)}) async-start(), calls=%async_computation.4 | async-start | bytes 4194304 | tf_op jit(solution)/shard_map/psum | solution.py:178
  119.0 2.8 %copy-start.24 = (f32[768,512]{0,1:T(8,128)S(1)}, f32[768,512]{0,1:T(8,128)}, u32[]{:S(2)}) copy-start(f32[768,512]{0,1:T(8,128)} %copy-done.23) | copy-start | bytes 4718596
  131.0 3.7 %copy-start.14 = (f32[12,3840]{1,0:T(8,128)S(1)}, f32[12,3840]{1,0:T(8,128)}, u32[]{:S(2)}) copy-start(f32[12,3840]{1,0:T(8,128)} %get-tuple-element.35) | copy-start | bytes 552964
  131.3 8.8 %slice-start = ((s8[7864320]{0:T(1024)(128)(4,1)}), s8[3670016]{0:T(1024)(128)(4,1)S(1)}, s32[]{:S(2)}) async-start(s8[7864320]{0:T(1024)(128)(4,1)} %bitcast.181), calls=%async_computation.5 | async-start | bytes 7340032
  134.7 5.4 %slice-start.1 = ((s8[7864320]{0:T(1024)(128)(4,1)}), s8[4194304]{0:T(1024)(128)(4,1)S(1)}, s32[]{:S(2)}) async-start(s8[7864320]{0:T(1024)(128)(4,1)} %bitcast.181), calls=%async_computation.6 | async-start | bytes 8388608
  142.2 17.1 %copy-start.19 = (s32[512,1]{0,1:T(1,128)S(1)}, s32[512,1]{0,1:T(1,128)}, u32[]{:S(2)}) copy-start(s32[512,1]{0,1:T(1,128)} %copy-done.18) | copy-start | bytes 6148
  142.2 8.3 %collective-permute-start.2 = (f32[32,1280]{1,0:T(8,128)S(1)}, f32[32,1280]{1,0:T(8,128)S(1)}, u32[]{:S(2)}, u32[]{:S(2)}) collective-permute-start(f32[32,1280]{1,0:T(8,128)S(1)} %get-tuple-element.33), channel_id=1, source_target_pairs={{0,4},{4,8},{8,12},{12,16},{16,20},{20,24},{24,28},{1,5},{5,9},{9,... | collective-permute-start | bytes 491528 | tf_op jit(solution)/shard_map/ppermute | solution.py:18
  145.9 7.2 %collective-permute-start.3 = (f32[32,1280]{1,0:T(8,128)S(1)}, f32[32,1280]{1,0:T(8,128)S(1)}, u32[]{:S(2)}, u32[]{:S(2)}) collective-permute-start(f32[32,1280]{1,0:T(8,128)S(1)} %get-tuple-element.34), channel_id=1, source_target_pairs={{4,0},{8,4},{12,8},{16,12},{20,16},{24,20},{28,24},{5,1},{9,5},{13... | collective-permute-start | bytes 491528 | tf_op jit(solution)/shard_map/ppermute | solution.py:20
  154.1 45.9 %all-to-all-start.3 = ((f32[32,8,160]{2,0,1:T(8,128)}), f32[32,8,160]{2,0,1:T(8,128)S(1)}, u32[]{:S(2)}, u32[]{:S(2)}) async-start(f32[32,8,160]{2,0,1:T(8,128)} %copy.99), calls=%async_computation.3 | async-start | bytes 524288 | tf_op jit(solution)/shard_map/all_to_all | solution.py:183
  (12 other events, 25.4 us)
Sparse Core Ops, SparseCore 0:
  125.7 134.9 all-reduce.2
